TPU v7x, 256 devices: a whole 4x4x8 slice. The times are simulated.
256 devices in a mesh: vocab: 32 (over y_hi, z, core), width: 8 (over x, y_lo).
Axes of the slice: x: 4, y: 4 (y_hi: 2, y_lo: 2; y = y_hi * 2 + y_lo), z: 8, core: 2. Of those that a mesh axis runs over, the one named last changes fastest.
Arguments:
- hidden: bfloat16 [256, 4608], P('vocab', 'width'), may hold values from -72 to 72
- pre_gain: float32 [4608], P('width'), may hold values from 0.1 to 1.9
- post_gain: float32 [4608], P('width'), may hold values from 0.1 to 1.9
- final_gain: float32 [4608], P('width'), may hold values from 0.1 to 1.9
- gate_weight: bfloat16 [4608, 18432], P('width', 'vocab'), may hold values from -0.09375 to 0.09375
- up_weight: bfloat16 [4608, 18432], P('width', 'vocab'), may hold values from -0.09375 to 0.09375
- down_weight: bfloat16 [18432, 4608], P('vocab', 'width'), may hold values from -2 to 2
- head_weight: bfloat16 [4608, 131072], P('width', 'vocab'), may hold values from -0.25 to 0.25
- token_ids: int32 [256], replicated, may hold values from 0 to 131071
- rewards: float32 [32], replicated, may hold values from -3 to 3
Outputs:
- grad_hidden: bfloat16 [256, 4608], P('vocab', 'width')
- grad_gate: bfloat16 [4608, 18432], P('width', 'vocab')
- grad_up: bfloat16 [4608, 18432], P('width', 'vocab')
- grad_down: bfloat16 [18432, 4608], P('vocab', 'width')
- grad_head: bfloat16 [4608, 131072], P('width', 'vocab')
- loss: float32 [], replicated
All inputs are finite; a program needn't handle non-finite values.
Results may differ from a plain program's by a relative error of at most 0.013.
Values may be sent and summed in bfloat16 or wider, within the bound.
No kernel may reach another device: no remote copies, remote signals or barrier semaphores. Data moves between devices by JAX's collectives and lax.ppermute only.
A program may use at most 64 MiB of HBM per device.

v0:
```python
import math
import jax
import jax.numpy as jnp
from jax import lax
from jax.sharding import PartitionSpec as P

CAP = 30
EPS = 1e-06
ROOT_TWO_PI = math.sqrt(2.0 / math.pi)


def gelu_value(value):
    inner = ROOT_TWO_PI * (value + 0.044715 * value * value * value)
    return 0.5 * value * (1.0 + jnp.tanh(inner))


def gelu_slope(value):
    bent = jnp.tanh(ROOT_TWO_PI * (value + 0.044715 * value * value * value))
    return 0.5 * (1.0 + bent) + 0.5 * value * (1.0 - bent * bent) * ROOT_TWO_PI * (
        1.0 + 3.0 * 0.044715 * value * value
    )


def contract(left, right, left_dim, right_dim):
    return lax.dot_general(
        left, right, (((left_dim,), (right_dim,)), ((), ())), preferred_element_type=jnp.float32
    )


def shards(
    hidden,
    pre_gain,
    post_gain,
    final_gain,
    gate_weight,
    up_weight,
    down_weight,
    head_weight,
    token_ids,
    rewards,
):
    tok_dev = hidden.shape[0]
    width_dev = hidden.shape[1]
    model = width_dev * lax.axis_size("width")
    vocab_index = lax.axis_index("vocab")
    width_index = lax.axis_index("width")
    own_start = vocab_index * tok_dev
    gathered = lax.all_gather(hidden, "vocab", axis=0, tiled=True)
    inputs = gathered.astype(jnp.float32)
    squares_pre = lax.psum(jnp.sum(inputs * inputs, axis=1), "width")
    scale_pre = lax.rsqrt(squares_pre / model + EPS)[:, None]
    normed = (inputs * scale_pre * pre_gain).astype(jnp.bfloat16)
    gate_part = jnp.dot(normed, gate_weight, preferred_element_type=jnp.float32)
    upward_part = jnp.dot(normed, up_weight, preferred_element_type=jnp.float32)
    gate, upward = lax.psum((gate_part, upward_part), "width")
    gelu_gate = gelu_value(gate)
    active = (gelu_gate * upward).astype(jnp.bfloat16)
    branch = lax.psum(jnp.dot(active, down_weight, preferred_element_type=jnp.float32), "vocab")
    branch_gain = branch * post_gain
    squares_post = lax.psum(jnp.sum(branch * branch, axis=1), "width")
    scale_post = lax.rsqrt(squares_post / model + EPS)[:, None]
    resid = inputs + scale_post * branch_gain
    squares_final = lax.psum(jnp.sum(resid * resid, axis=1), "width")
    scale_final = lax.rsqrt(squares_final / model + EPS)[:, None]
    final = (resid * scale_final * final_gain).astype(jnp.bfloat16)
    vocab_dev = head_weight.shape[1]
    sub_rows = vocab_dev // lax.axis_size("width")
    columns = head_weight
    logits = lax.psum_scatter(
        contract(columns, final, 0, 1), "width", scatter_dimension=0, tiled=True
    )
    capped = CAP * jnp.tanh(logits / CAP)
    first_column = vocab_index * vocab_dev + width_index * sub_rows
    column_ids = first_column + jnp.arange(sub_rows, dtype=jnp.int32)
    hits = column_ids[:, None] == token_ids[None, :]
    total, target = lax.psum(
        (jnp.sum(jnp.exp(capped - CAP), axis=0), jnp.sum(jnp.where(hits, capped, 0.0), axis=0)),
        ("vocab", "width"),
    )
    lognorm = CAP + jnp.log(total)
    logprob = target - lognorm
    weights = jnp.repeat(rewards, token_ids.shape[0] // rewards.shape[0])
    loss = -jnp.mean(weights * logprob)
    prob = jnp.exp(capped - lognorm[None, :])
    slope = 1.0 - (capped / CAP) ** 2
    delta = (-weights[None, :] * (hits.astype(jnp.float32) - prob) * slope).astype(jnp.bfloat16)
    piece = lax.all_gather(delta, "width", axis=0, tiled=True)
    columns = head_weight
    block = contract(final, piece, 0, 1)
    grad_cols = block
    grad_rows = contract(piece, columns, 0, 1)
    grad_cols, grad_rows = (grad_cols, grad_rows)
    grad_head = grad_cols.astype(jnp.bfloat16)
    grad_final = lax.psum(grad_rows, "vocab")
    weighted = grad_final * final_gain
    back_final = lax.psum(jnp.sum(weighted * resid, axis=1), "width")[:, None]
    grad_resid = scale_final * weighted - resid * scale_final**3 * back_final / model
    weighted_post = grad_resid * post_gain
    back_post = lax.psum(jnp.sum(weighted_post * branch, axis=1), "width")[:, None]
    grad_branch = (
        scale_post * weighted_post - branch * scale_post**3 * back_post / model
    ).astype(jnp.bfloat16)
    resid_rows = lax.dynamic_slice_in_dim(grad_resid, own_start, tok_dev, 0)
    grad_down = contract(active, grad_branch, 0, 0).astype(jnp.bfloat16)
    grad_active = lax.psum(contract(grad_branch, down_weight, 1, 1), "width")
    grad_gate_in = (grad_active * upward * gelu_slope(gate)).astype(jnp.bfloat16)
    grad_up_in = (grad_active * gelu_gate).astype(jnp.bfloat16)
    grad_gate = contract(normed, grad_gate_in, 0, 0).astype(jnp.bfloat16)
    grad_up = contract(normed, grad_up_in, 0, 0).astype(jnp.bfloat16)
    grad_normed = lax.psum_scatter(
        contract(grad_gate_in, gate_weight, 1, 1) + contract(grad_up_in, up_weight, 1, 1),
        "vocab",
        scatter_dimension=0,
        tiled=True,
    )
    own_inputs = hidden.astype(jnp.float32)
    own_scale = lax.dynamic_slice_in_dim(scale_pre, own_start, tok_dev, 0)
    weighted_pre = grad_normed * pre_gain
    back_pre = lax.psum(jnp.sum(weighted_pre * own_inputs, axis=1), "width")[:, None]
    grad_hidden = (
        resid_rows + own_scale * weighted_pre - own_inputs * own_scale**3 * back_pre / model
    ).astype(jnp.bfloat16)
    return (grad_hidden, grad_gate, grad_up, grad_down, grad_head, loss)


def solution(mesh):
    return jax.shard_map(
        shards,
        mesh=mesh,
        in_specs=(
            P("vocab", "width"),
            P("width"),
            P("width"),
            P("width"),
            P("width", "vocab"),
            P("width", "vocab"),
            P("vocab", "width"),
            P("width", "vocab"),
            P(),
            P(),
        ),
        out_specs=(
            P("vocab", "width"),
            P("width", "vocab"),
            P("width", "vocab"),
            P("vocab", "width"),
            P("width", "vocab"),
            P(),
        ),
        check_vma=False,
    )
```

profile of v0, /device:TPU:16, one launch (start us, length us, event | category | flops | bytes accessed | tf_op | source)
XLA Modules:
  0.0 1352.1 jit_solution(14111036055207850782)
XLA Ops:
  7.2 43.3 %all_gather.6 = bf16[256,576]{1,0:T(8,128)(2,1)S(1)} all-gather(bf16[8,576]{1,0:T(8,128)(2,1)} %param.10), channel_id=1, replica_groups=mesh['vocab'=32,'width'=8] {'vocab'}, dimensions={0}, use_global_device_ids=true | all-gather | bytes 304128 | tf_op jit(solution)/shard_map/all_gather | solution.py:48
  50.6 20.3 %psum.91 = f32[256]{0:T(256)S(1)} all-reduce(f32[256]{0:T(256)S(1)} %fusion), channel_id=1, replica_groups=mesh['vocab'=32,'width'=8] {'width'}, use_global_device_ids=true, to_apply=%region_1.0 | all-reduce | flops 256 | bytes 2048 | tf_op jit(solution)/shard_map/psum | solution.py:50
  71.0 2.5 fusion.23
  73.5 2.5 fusion.25
  76.0 77.8 %all-reduce.17.cloned.1.call-done = (f32[256,576]{0,1:T(8,128)}, f32[256,576]{0,1:T(8,128)}) async-done(((f32[256,576]{0,1:T(8,128)}, f32[256,576]{0,1:T(8,128)}), (f32[256,576]{0,1:T(8,128)}, f32[256,576]{0,1:T(8,128)})) %all-reduce.17.cloned.1.call-update) | async-done | bytes 1179664 | tf_op jit(solution)/shard_map/psum | solution.py:55
  153.8 1.4 multiply_convert_fusion.2
  156.0 1.3 fusion.27
  157.3 258.8 %all-reduce.9.cloned.1.call-done = f32[256,576]{1,0:T(8,128)} async-done(((f32[256,576]{1,0:T(8,128)}), f32[256,576]{1,0:T(8,128)}) %all-reduce.9.cloned.1.call-update) | async-done | bytes 589840 | tf_op jit(solution)/shard_map/psum | solution.py:58
  417.4 19.3 %psum.95 = f32[256]{0:T(256)S(1)} all-reduce(f32[256]{0:T(256)S(1)} %multiply_reduce_fusion.3), channel_id=1, replica_groups=mesh['vocab'=32,'width'=8] {'width'}, use_global_device_ids=true, to_apply=%region_6.0 | all-reduce | flops 256 | bytes 2048 | tf_op jit(solution)/shard_map/psum | solution.py:60
  436.7 1.4 multiply_reduce_fusion.2
  438.0 16.0 %psum.96 = f32[256]{0:T(256)S(1)} all-reduce(f32[256]{0:T(256)S(1)} %get-tuple-element.34), channel_id=1, replica_groups=mesh['vocab'=32,'width'=8] {'width'}, use_global_device_ids=true, to_apply=%region_8.0 | all-reduce | flops 256 | bytes 2048 | tf_op jit(solution)/shard_map/psum | solution.py:63
  454.0 6.2 convolution_bitcast_fusion
  461.1 86.4 %reduce-scatter.3.cloned.1.call-done = f32[512,256]{0,1:T(8,128)} async-done(((f32[4096,256]{0,1:T(8,128)}), f32[512,256]{0,1:T(8,128)}) %reduce-scatter.3.cloned.1.call-update) | async-done | bytes 524304 | tf_op jit(solution)/shard_map/reduce_scatter | solution.py:69
  547.5 1.3 fusion.14
  548.8 75.9 %all-reduce.1 = (f32[256]{0:T(256)S(1)}, f32[256]{0:T(256)S(1)}) all-reduce(f32[256]{0:T(256)S(1)} %get-tuple-element.25, f32[256]{0:T(256)S(1)} %get-tuple-element.24), channel_id=1, replica_groups=mesh['vocab'=32,'width'=8] {'vocab','width'}, use_global_device_ids=true, to_apply=%region_11.12 | all-reduce | flops 512 | bytes 4096 | tf_op jit(solution)/shard_map/psum | solution.py:76
  625.4 2.0 fusion.13
  627.5 51.3 %all-gather.2.cloned.1.call-done = bf16[4096,256]{0,1:T(8,128)(2,1)} async-done(((bf16[512,256]{0,1:T(8,128)(2,1)}), bf16[4096,256]{0,1:T(8,128)(2,1)}) %all-gather.2.cloned.1.call-update) | async-done | bytes 2097168 | tf_op jit(solution)/shard_map/all_gather | solution.py:87
  678.8 5.6 fusion.28
  684.5 259.4 %all-reduce.11.cloned.1.call-done = f32[256,576]{1,0:T(8,128)} async-done(((f32[256,576]{1,0:T(8,128)}), f32[256,576]{1,0:T(8,128)}) %all-reduce.11.cloned.1.call-update) | async-done | bytes 589840 | tf_op jit(solution)/shard_map/psum | solution.py:94
  945.1 19.3 %psum.99 = f32[256]{0:T(256)S(1)} all-reduce(f32[256]{0:T(256)S(1)} %multiply_reduce_fusion.1), channel_id=1, replica_groups=mesh['vocab'=32,'width'=8] {'width'}, use_global_device_ids=true, to_apply=%region_14.15 | all-reduce | flops 256 | bytes 2048 | tf_op jit(solution)/shard_map/psum | solution.py:96
  964.4 2.3 multiply_reduce_fusion
  966.7 15.9 %psum.100 = f32[256]{0:T(256)S(1)} all-reduce(f32[256]{0:T(256)S(1)} %get-tuple-element.32), channel_id=1, replica_groups=mesh['vocab'=32,'width'=8] {'width'}, use_global_device_ids=true, to_apply=%region_16.17 | all-reduce | flops 256 | bytes 2048 | tf_op jit(solution)/shard_map/psum | solution.py:99
  982.6 1.3 subtract_convert_fusion
  987.4 72.3 %all-reduce.13.cloned.1.call-done = f32[256,576]{0,1:T(8,128)} async-done(((f32[256,576]{0,1:T(8,128)}), f32[256,576]{0,1:T(8,128)}) %all-reduce.13.cloned.1.call-update) | async-done | bytes 589840 | tf_op jit(solution)/shard_map/psum | solution.py:105
  1059.7 1.9 multiply_convert_fusion.1
  1063.8 5.3 convolution_convert_fusion
  1069.1 1.3 convolution_convert_fusion.1
  1070.4 1.4 convolution_convert_fusion.2
  1071.8 249.0 %all-reduce.15.cloned.1.call-done = f32[256,576]{0,1:T(8,128)} async-done(((f32[256,576]{0,1:T(8,128)}), f32[256,576]{0,1:T(8,128)}) %all-reduce.15.cloned.1.call-update) | async-done | bytes 589840
  1322.1 1.4 convolution_convert_fusion.3
  1323.5 19.2 %psum.102 = f32[8]{0:T(128)S(1)} all-reduce(f32[8]{0:T(128)S(1)} %fusion.20), channel_id=1, replica_groups=mesh['vocab'=32,'width'=8] {'width'}, use_global_device_ids=true, to_apply=%region_20.21 | all-reduce | flops 8 | bytes 64 | tf_op jit(solution)/shard_map/psum | solution.py:119
  1342.7 1.4 fusion.19
  (59 shorter events, 10.6 us)
Async XLA Ops:
  7.2 148.8 %copy-start = (bf16[576,576]{1,0:T(8,128)(2,1)S(1)}, bf16[576,576]{1,0:T(8,128)(2,1)}, u32[]{:S(2)}) copy-start(bf16[576,576]{1,0:T(8,128)(2,1)} %param.16) | copy-start | bytes 1990660
  7.2 146.6 %all-reduce.17.cloned.1.call-start = ((), (), s32[]{:S(2)}) async-start(), calls=%async_computation.7 | async-start | bytes 2359296 | tf_op jit(solution)/shard_map/psum | solution.py:55
  71.0 365.7 %copy-start.9 = (f32[576]{0:T(1024)S(1)}, f32[576]{0:T(1024)}, u32[]{:S(2)}) copy-start(f32[576]{0:T(1024)} %param.12) | copy-start | bytes 6916
  73.5 380.6 %copy-start.6 = (f32[576]{0:T(1024)S(1)}, f32[576]{0:T(1024)}, u32[]{:S(2)}) copy-start(f32[576]{0:T(1024)} %param.13) | copy-start | bytes 6916
  76.0 340.2 %all-reduce.9.cloned.1.call-start = ((), (), s32[]{:S(2)}) async-start(), calls=%async_computation.1 | async-start | bytes 1310720 | tf_op jit(solution)/shard_map/psum | solution.py:58
  155.2 0.7 copy-start.4
  157.3 390.2 %reduce-scatter.3.cloned.1.call-start = ((), (), s32[]{:S(2)}) async-start(), calls=%async_computation.2 | async-start | bytes 4718592 | tf_op jit(solution)/shard_map/reduce_scatter | solution.py:69
  460.2 0.7 copy-start.11
  460.2 87.3 %copy-start.10 = (s32[256]{0:T(256)S(1)}, s32[256]{0:T(256)}, u32[]{:S(2)}) copy-start(s32[256]{0:T(256)} %param.18) | copy-start | bytes 3076
  460.2 218.6 %all-gather.2.cloned.1.call-start = ((), (), s32[]{:S(2)}) async-start(), calls=%async_computation.3 | async-start | bytes 2359296 | tf_op jit(solution)/shard_map/all_gather | solution.py:87
  627.4 337.0 %copy-start.1 = (f32[256,576]{1,0:T(8,128)S(1)}, f32[256,576]{1,0:T(8,128)}, u32[]{:S(2)}) copy-start(f32[256,576]{1,0:T(8,128)} %all-reduce.9.cloned.1.call-done) | copy-start | bytes 1769476
  627.4 316.5 %all-reduce.11.cloned.1.call-start = ((), (), s32[]{:S(2)}) async-start(), calls=%async_computation.4 | async-start | bytes 1310720 | tf_op jit(solution)/shard_map/psum | solution.py:94
  684.4 301.0 %copy-start.12 = (u32[256]{0:T(256)S(1)}, u32[256]{0:T(256)}, u32[]{:S(2)}) copy-start(u32[256]{0:T(256)} %constant.59) | copy-start | bytes 3076
  684.5 375.2 %all-reduce.13.cloned.1.call-start = ((), (), s32[]{:S(2)}) async-start(), calls=%async_computation.5 | async-start | bytes 1179648 | tf_op jit(solution)/shard_map/psum | solution.py:105
  964.4 97.2 %copy-start.2 = (bf16[576,576]{1,0:T(8,128)(2,1)S(1)}, bf16[576,576]{1,0:T(8,128)(2,1)}, u32[]{:S(2)}) copy-start(bf16[576,576]{1,0:T(8,128)(2,1)} %param.14) | copy-start | bytes 1990660
  985.2 335.5 %all-reduce.15.cloned.1.call-start = ((), (), s32[]{:S(2)}) async-start(), calls=%async_computation.6 | async-start | bytes 1179648
  1059.7 2.5 copy-start.3
  1063.7 5.4 copy-start.5
  1063.7 6.6 copy-start.7
  1063.8 258.2 %copy-start.8 = (bf16[8,576]{1,0:T(8,128)(2,1)S(1)}, bf16[8,576]{1,0:T(8,128)(2,1)}, u32[]{:S(2)}) copy-start(bf16[8,576]{1,0:T(8,128)(2,1)} %param.10) | copy-start | bytes 27652
Sparse Core Ops, SparseCore 0:
  76.1 77.6 all-reduce.16
  157.4 258.7 all-reduce.8
  460.4 87.0 reduce-scatter.2
  627.5 51.2 all-gather.1
  684.6 259.2 all-reduce.10
  985.3 74.3 all-reduce.12
  1063.8 256.8 all-reduce.14
where the time goes:
time: 1350 us
  waiting for transfers between devices  1060 us (79%)
  blocking collectives  229 us (17%)
  matrix products  29.8 us (2%)
  between operations  16.7 us (1%)
  other arithmetic  16.5 us (1%)
    psum x1, waiting for transfers between devices, shards(): grad_final = lax.psum(grad_rows, 'vocab')  259 us
    psum x1, waiting for transfers between devices, shards(): lax.psum(jnp.dot(active, down_weight, preferred_element_type=jnp.float32)...  259 us
    unnamed x8, waiting for transfers between devices  249 us
    reduce_scatter x1, waiting for transfers between devices, shards(): lax.psum_scatter(contract(columns, final, 0, 1), 'width', scatter_dimensi...  86.4 us
    psum x1, waiting for transfers between devices, shards(): gate, upward = lax.psum((gate_part, upward_part), 'width')  77.8 us
    psum x1, blocking collectives, shards(): lax.psum((jnp.sum(jnp.exp(capped - CAP), axis=0), jnp.sum(jnp.where(hits,...  75.9 us
    psum x1, waiting for transfers between devices, shards(): grad_active = lax.psum(contract(grad_branch, down_weight, 1, 1), 'width')  72.3 us
    all_gather x1, waiting for transfers between devices, shards(): piece = lax.all_gather(delta, 'width', axis=0, tiled=True)  51.3 us
  transfers between devices with their start and end apart: 7, of which 7 were waited for; matrix products, arithmetic and copies ran while one was open for 1% of the time, Pallas kernels for 0%

commit v1 on v0

--- a/solution.py
+++ b/solution.py
@@ -7,6 +7,12 @@
 CAP = 30
 EPS = 1e-06
 ROOT_TWO_PI = math.sqrt(2.0 / math.pi)
+
+
+def finish_lines(matrix):
+    r2 = lax.all_gather(matrix, "vocab")
+    block_out = jnp.sum(r2, 0)
+    return block_out
 
 
 def gelu_value(value):
@@ -55,7 +61,7 @@
     gate, upward = lax.psum((gate_part, upward_part), "width")
     gelu_gate = gelu_value(gate)
     active = (gelu_gate * upward).astype(jnp.bfloat16)
-    branch = lax.psum(jnp.dot(active, down_weight, preferred_element_type=jnp.float32), "vocab")
+    branch = finish_lines(jnp.dot(active, down_weight, preferred_element_type=jnp.float32))
     branch_gain = branch * post_gain
     squares_post = lax.psum(jnp.sum(branch * branch, axis=1), "width")
     scale_post = lax.rsqrt(squares_post / model + EPS)[:, None]

time: 1350 us -> 1280 us (0.948)
  waiting for transfers between devices: 1060 us -> 962 us
  local copies, waits for them, and re-layouts: 4.32 us -> 20.8 us
    psum x1 -> x0, waiting for transfers between devices: 259 us -> none  [shards(): lax.psum(jnp.dot(active, down_weight, preferred_element_type=jnp.float32)...]
    all_gather x0 -> x1, waiting for transfers between devices: none -> 163 us  [finish_lines(): r2 = lax.all_gather(matrix, 'vocab')]
    unnamed x28 -> x25, local copies, waits for them, and re-layouts: 3.01 us -> 19.3 us
where the time goes in v1:
time: 1280 us
  waiting for transfers between devices  962 us (75%)
  blocking collectives  230 us (18%)
  matrix products  30.8 us (2%)
  other arithmetic  23.8 us (2%)
  local copies, waits for them, and re-layouts  20.8 us (2%)
  between operations  16.8 us (1%)
    psum x1, waiting for transfers between devices, shards(): grad_final = lax.psum(grad_rows, 'vocab')  259 us
    unnamed x8, waiting for transfers between devices  249 us
    all_gather x1, waiting for transfers between devices, finish_lines(): r2 = lax.all_gather(matrix, 'vocab')  163 us
    reduce_scatter x1, waiting for transfers between devices, shards(): lax.psum_scatter(contract(columns, final, 0, 1), 'width', scatter_dimensi...  88.8 us
    psum x1, waiting for transfers between devices, shards(): gate, upward = lax.psum((gate_part, upward_part), 'width')  77.7 us
    psum x1, blocking collectives, shards(): lax.psum((jnp.sum(jnp.exp(capped - CAP), axis=0), jnp.sum(jnp.where(hits,...  76.1 us
    psum x1, waiting for transfers between devices, shards(): grad_active = lax.psum(contract(grad_branch, down_weight, 1, 1), 'width')  72.6 us
    all_gather x1, waiting for transfers between devices, shards(): piece = lax.all_gather(delta, 'width', axis=0, tiled=True)  51.3 us
  transfers between devices with their start and end apart: 7, of which 7 were waited for; matrix products, arithmetic and copies ran while one was open for 1% of the time, Pallas kernels for 0%

profile of v1, /device:TPU:16, one launch (start us, length us, event | category | flops | bytes accessed | tf_op | source)
XLA Modules:
  0.0 1283.9 jit_solution(6386753980862892856)
XLA Ops:
  7.2 43.3 %all_gather.12 = bf16[256,576]{1,0:T(8,128)(2,1)S(1)} all-gather(bf16[8,576]{1,0:T(8,128)(2,1)} %param.10), channel_id=1, replica_groups=mesh['vocab'=32,'width'=8] {'vocab'}, dimensions={0}, use_global_device_ids=true | all-gather | bytes 304128 | tf_op jit(solution)/shard_map/all_gather | solution.py:54
  50.6 20.3 %psum.84 = f32[256]{0:T(256)S(1)} all-reduce(f32[256]{0:T(256)S(1)} %fusion), channel_id=1, replica_groups=mesh['vocab'=32,'width'=8] {'width'}, use_global_device_ids=true, to_apply=%region_1.0 | all-reduce | flops 256 | bytes 2048 | tf_op jit(solution)/shard_map/psum | solution.py:56
  71.0 2.5 fusion.25
  73.4 2.5 fusion.23
  76.0 77.7 %all-reduce.14.cloned.1.call-done = (f32[256,576]{0,1:T(8,128)}, f32[256,576]{0,1:T(8,128)}) async-done(((f32[256,576]{0,1:T(8,128)}, f32[256,576]{0,1:T(8,128)}), (f32[256,576]{0,1:T(8,128)}, f32[256,576]{0,1:T(8,128)})) %all-reduce.14.cloned.1.call-update) | async-done | bytes 1179664 | tf_op jit(solution)/shard_map/psum | solution.py:61
  153.7 1.4 multiply_convert_fusion.2
  156.5 163.3 %all-gather.6.cloned.1.call-done = f32[8192,576]{0,1:T(8,128)} async-done(((f32[256,576]{0,1:T(8,128)}), f32[8192,576]{0,1:T(8,128)}) %all-gather.6.cloned.1.call-update) | async-done | bytes 18874384 | tf_op jit(solution)/shard_map/all_gather | solution.py:13
  319.8 17.6 %copy.57 = f32[72,8,32,256]{3,2,1,0:T(8,128)} copy(f32[72,8,32,256]{3,1,2,0:T(8,128)} %bitcast.28) | data formatting | bytes 37748736
  337.4 9.7 bitcast_reduce_fusion
  347.4 19.3 %psum.87 = f32[256]{0:T(256)S(1)} all-reduce(f32[256]{0:T(256)S(1)} %multiply_reduce_fusion.3), channel_id=1, replica_groups=mesh['vocab'=32,'width'=8] {'width'}, use_global_device_ids=true, to_apply=%region_6.0 | all-reduce | flops 256 | bytes 2048 | tf_op jit(solution)/shard_map/psum | solution.py:66
  367.0 16.0 %psum.88 = f32[256]{0:T(256)S(1)} all-reduce(f32[256]{0:T(256)S(1)} %get-tuple-element.34), channel_id=1, replica_groups=mesh['vocab'=32,'width'=8] {'width'}, use_global_device_ids=true, to_apply=%region_8.0 | all-reduce | flops 256 | bytes 2048 | tf_op jit(solution)/shard_map/psum | solution.py:69
  383.0 6.2 convolution_bitcast_fusion
  389.5 88.8 %reduce-scatter.3.cloned.1.call-done = f32[512,256]{0,1:T(8,128)} async-done(((f32[4096,256]{0,1:T(8,128)}), f32[512,256]{0,1:T(8,128)}) %reduce-scatter.3.cloned.1.call-update) | async-done | bytes 524304 | tf_op jit(solution)/shard_map/reduce_scatter | solution.py:75
  478.2 1.3 fusion.14
  479.6 76.1 %all-reduce.1 = (f32[256]{0:T(256)S(1)}, f32[256]{0:T(256)S(1)}) all-reduce(f32[256]{0:T(256)S(1)} %get-tuple-element.25, f32[256]{0:T(256)S(1)} %get-tuple-element.24), channel_id=1, replica_groups=mesh['vocab'=32,'width'=8] {'vocab','width'}, use_global_device_ids=true, to_apply=%region_11.12 | all-reduce | flops 512 | bytes 4096 | tf_op jit(solution)/shard_map/psum | solution.py:82
  556.3 2.0 fusion.13
  558.4 51.3 %all-gather.4.cloned.1.call-done = bf16[4096,256]{0,1:T(8,128)(2,1)} async-done(((bf16[512,256]{0,1:T(8,128)(2,1)}), bf16[4096,256]{0,1:T(8,128)(2,1)}) %all-gather.4.cloned.1.call-update) | async-done | bytes 2097168 | tf_op jit(solution)/shard_map/all_gather | solution.py:93
  609.7 5.6 fusion.28
  615.5 259.1 %all-reduce.8.cloned.1.call-done = f32[256,576]{1,0:T(8,128)} async-done(((f32[256,576]{1,0:T(8,128)}), f32[256,576]{1,0:T(8,128)}) %all-reduce.8.cloned.1.call-update) | async-done | bytes 589840 | tf_op jit(solution)/shard_map/psum | solution.py:100
  875.8 19.4 %psum.91 = f32[256]{0:T(256)S(1)} all-reduce(f32[256]{0:T(256)S(1)} %multiply_reduce_fusion.1), channel_id=1, replica_groups=mesh['vocab'=32,'width'=8] {'width'}, use_global_device_ids=true, to_apply=%region_14.15 | all-reduce | flops 256 | bytes 2048 | tf_op jit(solution)/shard_map/psum | solution.py:102
  895.2 2.2 multiply_reduce_fusion
  897.4 15.9 %psum.92 = f32[256]{0:T(256)S(1)} all-reduce(f32[256]{0:T(256)S(1)} %get-tuple-element.32), channel_id=1, replica_groups=mesh['vocab'=32,'width'=8] {'width'}, use_global_device_ids=true, to_apply=%region_16.17 | all-reduce | flops 256 | bytes 2048 | tf_op jit(solution)/shard_map/psum | solution.py:105
  913.3 1.3 subtract_convert_fusion
  917.9 72.6 %all-reduce.10.cloned.1.call-done = f32[256,576]{0,1:T(8,128)} async-done(((f32[256,576]{0,1:T(8,128)}), f32[256,576]{0,1:T(8,128)}) %all-reduce.10.cloned.1.call-update) | async-done | bytes 589840 | tf_op jit(solution)/shard_map/psum | solution.py:111
  990.5 1.9 multiply_convert_fusion.1
  992.9 1.6 convolution_add_fusion
  995.6 5.3 convolution_convert_fusion
  1002.2 1.4 convolution_convert_fusion.2
  1003.6 249.0 %all-reduce.12.cloned.1.call-done = f32[256,576]{0,1:T(8,128)} async-done(((f32[256,576]{0,1:T(8,128)}), f32[256,576]{0,1:T(8,128)}) %all-reduce.12.cloned.1.call-update) | async-done | bytes 589840
  1253.9 1.4 convolution_convert_fusion.3
  1255.3 19.2 %psum.94 = f32[8]{0:T(128)S(1)} all-reduce(f32[8]{0:T(128)S(1)} %fusion.20), channel_id=1, replica_groups=mesh['vocab'=32,'width'=8] {'width'}, use_global_device_ids=true, to_apply=%region_20.21 | all-reduce | flops 8 | bytes 64 | tf_op jit(solution)/shard_map/psum | solution.py:125
  1274.6 1.4 fusion.19
  (58 shorter events, 10.6 us)
Async XLA Ops:
  7.2 147.9 %copy-start = (bf16[576,576]{1,0:T(8,128)(2,1)S(1)}, bf16[576,576]{1,0:T(8,128)(2,1)}, u32[]{:S(2)}) copy-start(bf16[576,576]{1,0:T(8,128)(2,1)} %param.16) | copy-start | bytes 1990660
  7.2 146.5 %all-reduce.14.cloned.1.call-start = ((), (), s32[]{:S(2)}) async-start(), calls=%async_computation.7 | async-start | bytes 2359296 | tf_op jit(solution)/shard_map/psum | solution.py:61
  75.9 243.9 %all-gather.6.cloned.1.call-start = ((), (), s32[]{:S(2)}) async-start(), calls=%async_computation.5 | async-start | bytes 19464192 | tf_op jit(solution)/shard_map/all_gather | solution.py:13
  155.1 164.7 %copy-start.2 = (bf16[256,576]{0,1:T(8,128)(2,1)}, bf16[256,576]{0,1:T(8,128)(2,1)S(1)}, u32[]{:S(2)}) copy-start(bf16[256,576]{0,1:T(8,128)(2,1)S(1)} %multiply_convert_fusion.2) | copy-start | bytes 884740
  156.4 321.8 %reduce-scatter.3.cloned.1.call-start = ((), (), s32[]{:S(2)}) async-start(), calls=%async_computation.1 | async-start | bytes 4718592 | tf_op jit(solution)/shard_map/reduce_scatter | solution.py:75
  337.4 29.3 %copy-start.7 = (f32[576]{0:T(1024)S(1)}, f32[576]{0:T(1024)}, u32[]{:S(2)}) copy-start(f32[576]{0:T(1024)} %param.12) | copy-start | bytes 6916
  337.4 45.6 %copy-start.4 = (f32[576]{0:T(1024)S(1)}, f32[576]{0:T(1024)}, u32[]{:S(2)}) copy-start(f32[576]{0:T(1024)} %param.13) | copy-start | bytes 6916
  382.9 6.3 copy-start.9
  382.9 95.3 %copy-start.8 = (s32[256]{0:T(256)S(1)}, s32[256]{0:T(256)}, u32[]{:S(2)}) copy-start(s32[256]{0:T(256)} %param.18) | copy-start | bytes 3076
  389.2 220.5 %all-gather.4.cloned.1.call-start = ((), (), s32[]{:S(2)}) async-start(), calls=%async_computation.2 | async-start | bytes 2359296 | tf_op jit(solution)/shard_map/all_gather | solution.py:93
  558.4 316.2 %all-reduce.8.cloned.1.call-start = ((), (), s32[]{:S(2)}) async-start(), calls=%async_computation.3 | async-start | bytes 1310720 | tf_op jit(solution)/shard_map/psum | solution.py:100
  615.4 300.6 %copy-start.10 = (u32[256]{0:T(256)S(1)}, u32[256]{0:T(256)}, u32[]{:S(2)}) copy-start(u32[256]{0:T(256)} %constant.59) | copy-start | bytes 3076
  615.4 375.1 %all-reduce.10.cloned.1.call-start = ((), (), s32[]{:S(2)}) async-start(), calls=%async_computation.4 | async-start | bytes 1179648 | tf_op jit(solution)/shard_map/psum | solution.py:111
  875.8 116.6 %copy-start.1 = (bf16[576,576]{1,0:T(8,128)(2,1)S(1)}, bf16[576,576]{1,0:T(8,128)(2,1)}, u32[]{:S(2)}) copy-start(bf16[576,576]{1,0:T(8,128)(2,1)} %param.14) | copy-start | bytes 1990660
  915.9 336.6 %all-reduce.12.cloned.1.call-start = ((), (), s32[]{:S(2)}) async-start(), calls=%async_computation.6 | async-start | bytes 1179648
  995.6 5.4 copy-start.3
  995.6 6.6 copy-start.5
  995.6 258.2 %copy-start.6 = (bf16[8,576]{1,0:T(8,128)(2,1)S(1)}, bf16[8,576]{1,0:T(8,128)(2,1)}, u32[]{:S(2)}) copy-start(bf16[8,576]{1,0:T(8,128)(2,1)} %param.10) | copy-start | bytes 27652
Sparse Core Ops, SparseCore 0:
  76.1 77.5 all-reduce.13
  156.8 162.9 all-gather.5
  389.3 88.8 reduce-scatter.2
  558.5 51.2 all-gather.3
  615.5 258.9 all-reduce.7
  916.0 74.4 all-reduce.9
  995.7 256.8 all-reduce.11
